TPU v7x, 512 devices: a whole 4x8x8 slice. The times are simulated.
512 devices in a mesh: seq: 32 (over y, x), head: 16 (over z, core).
Axes of the slice: x: 4, y: 8, z: 8, core: 2. Of those that a mesh axis runs over, the one named last changes fastest.
Arguments:
- queries: bfloat16 [8192, 8192], P('seq', 'head'), may hold values from -1.796875 to 1.796875
- key_rows: bfloat16 [8192, 8192], P('seq', 'head'), may hold values from -1.796875 to 1.796875
- value_rows: bfloat16 [8192, 8192], P('seq', 'head'), may hold values from -6 to 6
- level_table: float32 [64, 7, 64], P(None, None, 'head'), may hold values from 0.25 to 4
- level_index: int32 [8192, 7], P('seq'), may hold values from 0 to 63
- norm_gain: float32 [8192], replicated, may hold values from 0.5 to 1.5
- cotangent: bfloat16 [8192, 8192], P(('seq', 'head')), may hold values from -6 to 6
Outputs:
- normed: bfloat16 [8192, 8192], P(('seq', 'head'))
- grad_query: bfloat16 [8192, 8192], P('seq', 'head')
- grad_key: bfloat16 [8192, 8192], P('seq', 'head')
- grad_value: bfloat16 [8192, 8192], P('seq', 'head')
- grad_table: float32 [64, 7, 64], P(None, None, 'head')
- grad_gain: float32 [8192], replicated
All inputs are finite; a program needn't handle non-finite values.
Results may differ from a plain program's by a relative error of at most 0.014.
Values may be sent and summed in bfloat16 or wider, within the bound.
A program may use at most 64 MiB of HBM per device.

v0:
```python
import jax
import jax.numpy as jnp
from jax import lax
from jax.sharding import PartitionSpec as P

CH = 128
LEVELS = 7
TABLE = 64
EPSILON = 1e-06
HIGHEST = lax.Precision.HIGHEST


def swapped(value, axis, bit):
    mask = 2**bit
    pairs = [(source, source ^ mask) for source in range(lax.axis_size(axis))]
    return lax.ppermute(value, axis, pairs)


def bit_length_of(values, places):
    result = jnp.zeros_like(values)
    for exponent in range(places):
        result = result + (values >= 1 << exponent).astype(jnp.int32)
    return result


def level_mask(spans):
    row_ids = lax.broadcasted_iota(jnp.int32, (spans, spans), 0)
    col_ids = lax.broadcasted_iota(jnp.int32, (spans, spans), 1)
    lengths = bit_length_of(jnp.bitwise_xor(row_ids, col_ids), 16)
    stacked = [((lengths == 1) & (col_ids < row_ids)).astype(jnp.float32)]
    return jnp.stack(stacked)


def body(queries, key_rows, value_rows, level_table, level_index, norm_gain, cotangent):
    tok_dev = queries.shape[0]
    head_count = level_table.shape[2]
    head_width = queries.shape[1] // head_count
    spans = tok_dev // CH
    local_bits = spans.bit_length() - 1
    seq_bits = lax.axis_size("seq").bit_length() - 1
    cross_count = LEVELS - 1 - local_bits
    shard_id = lax.axis_index("seq")
    query_blocks = queries.reshape(spans, CH, head_count, head_width)
    key_blocks = key_rows.reshape(spans, CH, head_count, head_width)
    value_blocks = value_rows.reshape(spans, CH, head_count, head_width)
    onehot = (level_index[:, :, None] == jnp.arange(TABLE, dtype=jnp.int32)[None, None, :]).astype(
        jnp.float32
    )
    weights = jnp.einsum("tlx,xlh->tlh", onehot, level_table, precision=HIGHEST)
    weights = weights.reshape(spans, CH, LEVELS, head_count)
    span_states = jnp.einsum(
        "icha,ichb->ihab", key_blocks, value_blocks, preferred_element_type=jnp.float32
    )
    masks_local = level_mask(spans)
    intra_states = jnp.einsum("mij,jhab->imhab", masks_local, span_states, precision=HIGHEST)
    shard_total = jnp.sum(span_states, axis=0)
    state_zeros = jnp.zeros((cross_count, head_count, head_width, head_width), jnp.float32)
    shards_in = lax.all_gather(
        shard_total[None].astype(jnp.bfloat16), "seq", axis=0, tiled=True
    ).astype(jnp.float32)
    source = jnp.arange(shards_in.shape[0], dtype=jnp.int32)
    lengths = bit_length_of(jnp.bitwise_xor(source, shard_id), 16)
    slot_of = jnp.minimum(lengths + local_bits, LEVELS - 1) - local_bits - 1
    selector = (slot_of[:, None] == jnp.arange(cross_count, dtype=jnp.int32)[None, :]) & (
        source < shard_id
    )[:, None]
    cross_states = state_zeros + jnp.einsum(
        "sk,shab->khab", selector.astype(jnp.float32), shards_in, precision=HIGHEST
    )
    spread = jnp.broadcast_to(cross_states[None], (spans,) + cross_states.shape)
    level_states = jnp.concatenate([intra_states, spread], axis=1).astype(jnp.bfloat16)
    far_out = jnp.einsum(
        "icha,ilhab->iclhb", query_blocks, level_states, preferred_element_type=jnp.float32
    )
    row_ids = lax.broadcasted_iota(jnp.int32, (CH, CH), 0)
    col_ids = lax.broadcasted_iota(jnp.int32, (CH, CH), 1)
    causal = col_ids <= row_ids
    scores = jnp.einsum(
        "icha,inha->ihcn", query_blocks, key_blocks, preferred_element_type=jnp.float32
    )
    scores = jnp.where(causal, scores, 0.0)
    near_out = jnp.einsum(
        "ihcn,inhb->ichb",
        scores.astype(jnp.bfloat16),
        value_blocks,
        preferred_element_type=jnp.float32,
    )
    level_out = jnp.concatenate([near_out[:, :, None], far_out], axis=2)
    attn = jnp.sum(weights[..., None] * level_out, axis=2).astype(jnp.bfloat16)
    attn_rows = attn.reshape(tok_dev, head_count * head_width)
    token_attn = lax.all_to_all(attn_rows, "head", split_axis=0, concat_axis=1, tiled=True)
    attn_f = token_attn.astype(jnp.float32)
    inv_rms = lax.rsqrt(jnp.mean(attn_f * attn_f, axis=1, keepdims=True) + EPSILON)
    unit_rows = attn_f * inv_rms
    normed = (unit_rows * norm_gain).astype(jnp.bfloat16)
    grad_out = cotangent.astype(jnp.float32)
    scaled = grad_out * norm_gain
    grad_gain = lax.psum(jnp.sum(grad_out * unit_rows, axis=0), ("seq", "head"))
    grad_attn = (
        (scaled - unit_rows * jnp.mean(scaled * unit_rows, axis=1, keepdims=True)) * inv_rms
    ).astype(jnp.bfloat16)
    head_grad = lax.all_to_all(grad_attn, "head", split_axis=1, concat_axis=0, tiled=True)
    grad_blocks = head_grad.reshape(spans, CH, head_count, head_width)
    grad_f = grad_blocks.astype(jnp.float32)
    grad_weight = jnp.sum(level_out * grad_f[:, :, None], axis=4)
    along_values = jnp.einsum(
        "ichb,inhb->ihcn", grad_blocks, value_blocks, preferred_element_type=jnp.float32
    )
    first_weight = jnp.transpose(weights[:, :, 0, :], (0, 2, 1))[..., None]
    grad_scores = jnp.where(causal, along_values * first_weight, 0.0).astype(jnp.bfloat16)
    weighted_scores = jnp.where(causal, scores * first_weight, 0.0).astype(jnp.bfloat16)
    near_dq = jnp.einsum(
        "ihcn,inha->icha", grad_scores, key_blocks, preferred_element_type=jnp.float32
    )
    near_dk = jnp.einsum(
        "ihcn,icha->inha", grad_scores, query_blocks, preferred_element_type=jnp.float32
    )
    near_dv = jnp.einsum(
        "ihcn,ichb->inhb", weighted_scores, grad_blocks, preferred_element_type=jnp.float32
    )
    far_dq = jnp.einsum(
        "ichb,ilhab->iclha", grad_blocks, level_states, preferred_element_type=jnp.float32
    )
    grad_query = near_dq + jnp.sum(weights[:, :, 1:, :, None] * far_dq, axis=2)
    scaled_grad = (weights[:, :, 1:, :, None] * grad_f[:, :, None]).astype(jnp.bfloat16)
    query_grads = jnp.einsum(
        "icha,iclhb->ilhab", query_blocks, scaled_grad, preferred_element_type=jnp.float32
    )
    inner_grad = jnp.einsum(
        "mij,imhab->jhab", masks_local, query_grads[:, :local_bits], precision=HIGHEST
    )
    shard_grads = jnp.sum(query_grads[:, local_bits:], axis=0)
    cross_grad = jnp.zeros((head_count, head_width, head_width), jnp.float32)
    group_grads = shard_grads
    for bit_pos in range(seq_bits):
        partner = swapped(group_grads.astype(jnp.bfloat16), "seq", bit_pos).astype(
            group_grads.dtype
        )
        lower_half = 1.0 - jnp.bitwise_and(jnp.right_shift(shard_id, bit_pos), 1).astype(
            jnp.float32
        )
        level_slot = min(bit_pos, cross_count - 1)
        cross_grad = cross_grad + lower_half * partner[level_slot]
        group_grads = group_grads + partner
    key_state = (inner_grad + cross_grad[None]).astype(jnp.bfloat16)
    grad_key = near_dk + jnp.einsum(
        "jhab,jnhb->jnha", key_state, value_blocks, preferred_element_type=jnp.float32
    )
    grad_value = near_dv + jnp.einsum(
        "jhab,jnha->jnhb", key_state, key_blocks, preferred_element_type=jnp.float32
    )
    table_part = jnp.einsum(
        "tlx,tlh->xlh", onehot, grad_weight.reshape(tok_dev, LEVELS, head_count), precision=HIGHEST
    )
    grad_table = lax.psum(table_part, "seq")
    row_shape = (tok_dev, head_count * head_width)
    return (
        normed,
        grad_query.astype(jnp.bfloat16).reshape(row_shape),
        grad_key.astype(jnp.bfloat16).reshape(row_shape),
        grad_value.astype(jnp.bfloat16).reshape(row_shape),
        grad_table,
        grad_gain,
    )


def solution(mesh):
    placed = (
        P("seq", "head"),
        P("seq", "head"),
        P("seq", "head"),
        P(None, None, "head"),
        P("seq", None),
        P(),
        P(("seq", "head"), None),
    )
    return jax.shard_map(
        body,
        mesh=mesh,
        in_specs=placed,
        out_specs=(
            P(("seq", "head"), None),
            P("seq", "head"),
            P("seq", "head"),
            P("seq", "head"),
            P(None, None, "head"),
            P(),
        ),
        check_vma=False,
    )
```

profile of v0, /device:TPU:32, one launch (start us, length us, event | category | flops | bytes accessed | tf_op | source)
XLA Modules:
  0.0 519.8 jit_solution(9532326248119924726)
XLA Ops:
  7.2 1.1 reshape.150
  8.3 1.0 reshape.151
  9.3 0.9 fusion.135
  10.3 0.3 convolution_bitcast_fusion.6
  10.7 1.3 fusion.16
  12.0 0.2 copy.206
  12.3 0.3 convolution_select_fusion
  12.6 0.8 copy-done.5
  13.4 0.3 convolution_bitcast_fusion.5
  13.8 86.5 %all-gather.3.cloned.1.call-done = bf16[128,128,128]{2,1,0:T(8,128)(2,1)} async-done(((bf16[4,128,128]{2,1,0:T(8,128)(2,1)}), bf16[128,128,128]{2,1,0:T(8,128)(2,1)}) %all-gather.3.cloned.1.call-update) | async-done | bytes 4194320 | tf_op jit(solution)/shard_map/all_gather | solution.py:58
  100.3 4.5 fusion.5
  104.8 0.6 copy.205
  105.4 0.3 broadcast_in_dim.23
  105.8 1.0 copy-done.4
  106.8 0.6 convolution_bitcast_fusion.1
  107.4 1.7 copy-done.1
  109.1 0.5 multiply_reduce_fusion.1
  110.0 18.5 %all_to_all.26 = bf16[16,16,512]{2,1,0:T(8,128)(2,1)S(1)} all-to-all(bf16[16,16,512]{2,1,0:T(8,128)(2,1)S(1)} %convert_element_type.402), channel_id=1, replica_groups=mesh['seq'=32,'head'=16] {'head'}, dimensions={0} | all-to-all | bytes 524288 | tf_op jit(solution)/shard_map/all_to_all | solution.py:91
  128.8 0.4 fusion.22
  129.1 0.9 fusion.21
  130.0 0.7 copy.311
  130.7 3.5 all-to-all-start.1
  134.3 11.3 %all-to-all-done.1 = bf16[16,16,512]{2,0,1:T(8,128)(2,1)S(1)} async-done(((bf16[16,16,512]{2,0,1:T(8,128)(2,1)}), bf16[16,16,512]{2,0,1:T(8,128)(2,1)S(1)}, u32[]{:S(2)}, u32[]{:S(2)}) %all-to-all-start.1) | async-done | bytes 262176 | tf_op jit(solution)/shard_map/all_to_all | solution.py:102
  145.7 0.7 copy-done.10
  146.4 0.2 copy.224
  146.7 0.6 convolution_bitcast_fusion
  147.2 0.2 copy-done.8
  147.7 1.4 copy-done.3
  149.2 2.8 collective-permute-start
  152.0 16.3 %collective-permute-done = bf16[5,4,128,128]{2,3,0,1:T(8,128)(2,1)S(1)} collective-permute-done((bf16[5,4,128,128]{2,3,0,1:T(8,128)(2,1)S(1)}, bf16[5,4,128,128]{2,3,0,1:T(8,128)(2,1)S(1)}, u32[]{:S(2)}, u32[]{:S(2)}) %collective-permute-start) | collective-permute-done | bytes 655392 | tf_op jit(solution)/shard_map/ppermute | solution.py:16
  168.4 1.0 fusion.56
  169.4 4.0 collective-permute-start.1
  173.4 16.0 %collective-permute-done.1 = bf16[5,4,128,128]{2,3,0,1:T(8,128)(2,1)S(1)} collective-permute-done((bf16[5,4,128,128]{2,3,0,1:T(8,128)(2,1)}, bf16[5,4,128,128]{2,3,0,1:T(8,128)(2,1)S(1)}, u32[]{:S(2)}, u32[]{:S(2)}) %collective-permute-start.1) | collective-permute-done | bytes 655392 | tf_op jit(solution)/shard_map/ppermute | solution.py:16
  189.4 1.1 fusion.27
  190.5 4.0 collective-permute-start.2
  194.5 100.7 %psum.15 = f32[8192]{0:T(1024)} all-reduce(f32[8192]{0:T(1024)S(1)} %get-tuple-element.6), channel_id=1, replica_groups=mesh['seq'=32,'head'=16] {'seq','head'}, use_global_device_ids=true, to_apply=%region_9.10 | all-reduce | flops 8192 | bytes 65536 | tf_op jit(solution)/shard_map/psum | solution.py:98
  295.2 3.0 fusion.2
  298.2 2.0 copy.219
  300.3 1.3 fusion.11
  301.6 2.5 fusion.26
  304.0 2.5 collective-permute-start.3
  306.5 0.2 fusion.14
  306.8 0.2 copy.220
  307.0 0.7 copy.310
  307.7 0.6 multiply_reduce_fusion
  308.4 1.9 slice_bitcast_fusion
  310.3 2.0 copy.226
  312.3 25.5 %collective-permute-done.3 = bf16[5,4,128,128]{2,3,0,1:T(8,128)(2,1)} collective-permute-done((bf16[5,4,128,128]{2,3,0,1:T(8,128)(2,1)}, bf16[5,4,128,128]{2,3,0,1:T(8,128)(2,1)}, u32[]{:S(2)}, u32[]{:S(2)}) %collective-permute-start.3) | collective-permute-done | bytes 655392 | tf_op jit(solution)/shard_map/ppermute | solution.py:16
  337.8 2.6 add_convert_fusion
  340.4 4.2 collective-permute-start.4
  344.6 0.3 convolution_bitcast_fusion.7
  344.9 157.1 %psum.14 = f32[64,7,4]{0,2,1:T(4,128)} all-reduce(f32[64,7,4]{0,2,1:T(4,128)S(1)} %convolution_bitcast_fusion.7), channel_id=1, replica_groups=mesh['seq'=32,'head'=16] {'seq'}, use_global_device_ids=true, to_apply=%region_7.8 | all-reduce | flops 1792 | bytes 14336 | tf_op jit(solution)/shard_map/psum | solution.py:155
  502.0 2.1 fusion.61
  504.1 2.4 fusion.28
  506.8 1.2 convert_element_type.422
  508.0 1.2 convert_element_type.425
  509.2 1.1 fusion.31
  510.5 0.3 convolution_bitcast_fusion.2
  510.8 0.3 fusion.15
  511.1 0.3 copy-done.14
  511.4 0.3 fusion.13
  511.7 0.2 copy.231
  511.9 0.2 copy.235
  512.1 0.9 copy_bitcast_fusion
  (63 shorter events, 1.7 us)
Async XLA Ops:
  7.2 3.1 copy-start
  7.2 3.1 copy-start.19
  7.2 3.4 copy-start.17
  7.2 93.1 %all-gather.3.cloned.1.call-start = ((), (), s32[]{:S(2)}) async-start(), calls=%async_computation.2 | async-start | bytes 4325376 | tf_op jit(solution)/shard_map/all_gather | solution.py:58
  12.2 93.5 %copy-start.15 = (bf16[2,1,4,128,128]{3,4,1,2,0:T(8,128)(2,1)}, bf16[2,1,4,128,128]{3,4,1,2,0:T(8,128)(2,1)S(1)}, u32[]{:S(2)}) copy-start(bf16[2,1,4,128,128]{3,4,1,2,0:T(8,128)(2,1)S(1)} %copy.206) | copy-start | bytes 786436
  12.6 0.8 copy-start.5
  13.8 93.6 %copy-start.6 = (f32[2,128,1,4,128]{1,4,2,3,0:T(8,128)}, f32[2,128,1,4,128]{1,4,2,3,0:T(8,128)S(1)}, u32[]{:S(2)}) copy-start(f32[2,128,1,4,128]{1,4,2,3,0:T(8,128)S(1)} %convolution_bitcast_fusion.5) | copy-start | bytes 1572868
  105.8 1.0 copy-start.4
  107.4 1.7 copy-start.1
  109.8 18.9 %copy-start.16 = (bf16[16,8192]{1,0:T(8,128)(2,1)S(1)}, bf16[16,8192]{1,0:T(8,128)(2,1)}, u32[]{:S(2)}) copy-start(bf16[16,8192]{1,0:T(8,128)(2,1)} %param.13) | copy-start | bytes 786436
  109.9 18.9 %copy-start.18 = (f32[8192]{0:T(1024)S(1)}, f32[8192]{0:T(1024)}, u32[]{:S(2)}) copy-start(f32[8192]{0:T(1024)} %param.12) | copy-start | bytes 98308
  130.7 14.9 %all-to-all-start.1 = ((bf16[16,16,512]{2,0,1:T(8,128)(2,1)}), bf16[16,16,512]{2,0,1:T(8,128)(2,1)S(1)}, u32[]{:S(2)}, u32[]{:S(2)}) async-start(bf16[16,16,512]{2,0,1:T(8,128)(2,1)} %bitcast.93), calls=%async_computation.1 | async-start | bytes 524288 | tf_op jit(solution)/shard_map/all_to_all | solution.py:102
  145.7 0.7 copy-start.10
  146.6 0.8 copy-start.8
  147.5 1.6 copy-start.3
  149.2 19.2 %collective-permute-start = (bf16[5,4,128,128]{2,3,0,1:T(8,128)(2,1)S(1)}, bf16[5,4,128,128]{2,3,0,1:T(8,128)(2,1)S(1)}, u32[]{:S(2)}, u32[]{:S(2)}) collective-permute-start(bf16[5,4,128,128]{2,3,0,1:T(8,128)(2,1)S(1)} %convert_element_type.415), channel_id=1, source_target_pairs={{0,16},{16,0},{32,48},{48,32},{64,80},{80,64},{96,112},{112,96},{1... | collective-permute-start | bytes 1966088 | tf_op jit(solution)/shard_map/ppermute | solution.py:16
  169.4 20.0 %collective-permute-start.1 = (bf16[5,4,128,128]{2,3,0,1:T(8,128)(2,1)}, bf16[5,4,128,128]{2,3,0,1:T(8,128)(2,1)S(1)}, u32[]{:S(2)}, u32[]{:S(2)}) collective-permute-start(bf16[5,4,128,128]{2,3,0,1:T(8,128)(2,1)} %fusion.56), channel_id=1, source_target_pairs={{0,32},{16,48},{32,0},{48,16},{64,96},{80,112},{96,64},{112,80},{1... | collective-permute-start | bytes 1966088 | tf_op jit(solution)/shard_map/ppermute | solution.py:16
  190.5 111.1 %collective-permute-start.2 = (bf16[5,4,128,128]{2,3,0,1:T(8,128)(2,1)}, bf16[5,4,128,128]{2,3,0,1:T(8,128)(2,1)}, u32[]{:S(2)}, u32[]{:S(2)}) collective-permute-start(bf16[5,4,128,128]{2,3,0,1:T(8,128)(2,1)} %fusion.27), channel_id=1, source_target_pairs={{0,64},{16,80},{32,96},{48,112},{64,0},{80,16},{96,32},{112,48},{1... | collective-permute-start | bytes 1966088 | tf_op jit(solution)/shard_map/ppermute | solution.py:16
  301.5 5.0 copy-start.13
  301.6 5.0 copy-start.12
  301.6 6.1 %copy-start.2 = (f32[2,128,6,4,128]{1,4,2,3,0:T(8,128)S(1)}, f32[2,128,6,4,128]{1,4,2,3,0:T(8,128)}, u32[]{:S(2)}) copy-start(f32[2,128,6,4,128]{1,4,2,3,0:T(8,128)} %copy-done.1) | copy-start | bytes 9437188
  304.0 3.7 copy-start.7
  304.0 3.7 copy-start.9
  304.0 33.8 %collective-permute-start.3 = (bf16[5,4,128,128]{2,3,0,1:T(8,128)(2,1)}, bf16[5,4,128,128]{2,3,0,1:T(8,128)(2,1)}, u32[]{:S(2)}, u32[]{:S(2)}) collective-permute-start(bf16[5,4,128,128]{2,3,0,1:T(8,128)(2,1)} %fusion.26), channel_id=1, source_target_pairs={{0,128},{16,144},{32,160},{48,176},{64,192},{80,208},{96,224},{112... | collective-permute-start | bytes 1966088 | tf_op jit(solution)/shard_map/ppermute | solution.py:16
  340.4 168.8 %collective-permute-start.4 = (bf16[5,4,128,128]{2,3,0,1:T(8,128)(2,1)}, bf16[5,4,128,128]{2,3,0,1:T(8,128)(2,1)}, u32[]{:S(2)}, u32[]{:S(2)}) collective-permute-start(bf16[5,4,128,128]{2,3,0,1:T(8,128)(2,1)} %add_convert_fusion), channel_id=1, source_target_pairs={{0,256},{16,272},{32,288},{48,304},{64,320},{80,336},{96,352},{112... | collective-permute-start | bytes 1966088 | tf_op jit(solution)/shard_map/ppermute | solution.py:16
  509.2 1.5 copy-start.11
  510.4 1.0 copy-start.14
Sparse Core Ops, SparseCore 0:
  11.8 88.4 all-gather.2
where the time goes:
time: 521 us; the launch traced here: 520 us
  blocking collectives  276 us (53%)
  waiting for transfers between devices  156 us (30%)
  starting transfers between devices  21.1 us (4%)
  local copies, waits for them, and re-layouts  19.3 us (4%)
  matrix products  19 us (4%)
  between operations  14.6 us (3%)
  other arithmetic  13.9 us (3%)
    psum x1, blocking collectives, body(): grad_table = lax.psum(table_part, 'seq')  157 us
    psum x1, blocking collectives, body(): grad_gain = lax.psum(jnp.sum(grad_out * unit_rows, axis=0), ('seq', 'head'))  101 us
    all_gather x1, waiting for transfers between devices, body(): lax.all_gather(shard_total[None].astype(jnp.bfloat16), 'seq', axis=0, til...  86.5 us
    ppermute x5, waiting for transfers between devices, swapped(): return lax.ppermute(value, axis, pairs)  57.8 us
    all_to_all x1, blocking collectives, body(): lax.all_to_all(attn_rows, 'head', split_axis=0, concat_axis=1, tiled=True)  18.5 us
    ppermute x5, starting transfers between devices, swapped(): return lax.ppermute(value, axis, pairs)  17.5 us
    all_to_all x1, waiting for transfers between devices, body(): lax.all_to_all(grad_attn, 'head', split_axis=1, concat_axis=0, tiled=True)  11.3 us
  transfers between devices with their start and end apart: 7, of which 5 were waited for; matrix products, arithmetic and copies ran while one was open for 4% of the time, Pallas kernels for 0%

commit v1 on v0

--- a/solution.py
+++ b/solution.py
@@ -152,7 +152,11 @@
     table_part = jnp.einsum(
         "tlx,tlh->xlh", onehot, grad_weight.reshape(tok_dev, LEVELS, head_count), precision=HIGHEST
     )
-    grad_table = lax.psum(table_part, "seq")
+    grad_table = table_part
+    for hop in (1, 2, 4, 8, 16):
+        grad_table = grad_table + lax.ppermute(
+            grad_table, "seq", [(dev, dev ^ hop) for dev in range(32)]
+        )
     row_shape = (tok_dev, head_count * head_width)
     return (
         normed,

time: 521 us -> 402 us (0.77)
  the two profiles are of different devices: /device:TPU:32 before, /device:TPU:1 now
where the time goes in v1:
time: 402 us; the launch traced here: 401 us
  waiting for transfers between devices  177 us (44%)
  blocking collectives  123 us (31%)
  starting transfers between devices  37.7 us (9%)
  local copies, waits for them, and re-layouts  16.7 us (4%)
  other arithmetic  16.6 us (4%)
  matrix products  15.2 us (4%)
  between operations  14.7 us (4%)
    psum x1, blocking collectives, body(): grad_gain = lax.psum(jnp.sum(grad_out * unit_rows, axis=0), ('seq', 'head'))  101 us
    all_gather x1, waiting for transfers between devices, body(): lax.all_gather(shard_total[None].astype(jnp.bfloat16), 'seq', axis=0, til...  87.9 us
    ppermute x5, waiting for transfers between devices, swapped(): return lax.ppermute(value, axis, pairs)  48.2 us
    ppermute x5, waiting for transfers between devices, body(): lax.ppermute(grad_table, 'seq', [(dev, dev ^ hop) for dev in range(32)])  29.6 us
    all_to_all x1, blocking collectives, body(): lax.all_to_all(attn_rows, 'head', split_axis=0, concat_axis=1, tiled=True)  22.1 us
    ppermute x5, starting transfers between devices, body(): lax.ppermute(grad_table, 'seq', [(dev, dev ^ hop) for dev in range(32)])  17.9 us
    ppermute x5, starting transfers between devices, swapped(): return lax.ppermute(value, axis, pairs)  16.3 us
    all_to_all x1, waiting for transfers between devices, body(): lax.all_to_all(grad_attn, 'head', split_axis=1, concat_axis=0, tiled=True)  11.1 us
  transfers between devices with their start and end apart: 12, of which 7 were waited for; matrix products, arithmetic and copies ran while one was open for 6% of the time, Pallas kernels for 0%

profile of v1, /device:TPU:1, one launch (start us, length us, event | category | flops | bytes accessed | tf_op | source)
XLA Modules:
  0.0 401.0 jit_solution(689504358488497827)
XLA Ops:
  7.2 1.1 reshape.150
  8.3 1.0 reshape.151
  9.3 0.9 fusion.135
  10.3 0.3 convolution_bitcast_fusion.6
  10.7 1.3 fusion.16
  12.3 0.3 convolution_select_fusion
  12.6 0.8 copy-done.5
  13.5 0.3 convolution_bitcast_fusion.5
  13.8 87.9 %all-gather.3.cloned.1.call-done = bf16[128,128,128]{2,1,0:T(8,128)(2,1)} async-done(((bf16[4,128,128]{2,1,0:T(8,128)(2,1)}), bf16[128,128,128]{2,1,0:T(8,128)(2,1)}) %all-gather.3.cloned.1.call-update) | async-done | bytes 4194320 | tf_op jit(solution)/shard_map/all_gather | solution.py:58
  101.7 4.5 %fusion.5 = bf16[5,4,128,128]{3,0,2,1:T(8,128)(2,1)S(1)} fusion(bf16[32,4,128,128]{3,2,1,0:T(8,128)(2,1)} %bitcast.98, s32[32]{0:T(128)S(1)} %fusion.97, pred[32]{0:T(512)(128)(4,1)S(1)} %iota_compare_fusion.5), kind=kOutput, calls=%fused_computation.14 | convolution fusion | flops 21299520 | bytes 4849824 | tf_op jit(solution)/shard_map/sk,shab->khab/dot_general | solution.py:67
  106.3 0.6 copy.205
  106.9 0.3 broadcast_in_dim.23
  107.2 1.1 copy-done.3
  108.3 0.6 convolution_bitcast_fusion.1
  108.9 1.7 copy-done.1
  110.5 0.5 multiply_reduce_fusion.1
  111.4 22.1 %all_to_all.26 = bf16[16,16,512]{2,1,0:T(8,128)(2,1)S(1)} all-to-all(bf16[16,16,512]{2,1,0:T(8,128)(2,1)S(1)} %convert_element_type.402), channel_id=1, replica_groups=mesh['seq'=32,'head'=16] {'head'}, dimensions={0} | all-to-all | bytes 524288 | tf_op jit(solution)/shard_map/all_to_all | solution.py:91
  133.8 0.4 fusion.22
  134.2 0.9 fusion.21
  135.1 0.7 copy.311
  135.8 3.4 all-to-all-start.1
  139.3 11.1 %all-to-all-done.1 = bf16[16,16,512]{2,0,1:T(8,128)(2,1)S(1)} async-done(((bf16[16,16,512]{2,0,1:T(8,128)(2,1)}), bf16[16,16,512]{2,0,1:T(8,128)(2,1)S(1)}, u32[]{:S(2)}, u32[]{:S(2)}) %all-to-all-start.1) | async-done | bytes 262176 | tf_op jit(solution)/shard_map/all_to_all | solution.py:102
  150.5 0.7 copy-done.9
  151.4 0.6 convolution_bitcast_fusion
  152.4 1.4 copy-done.2
  153.9 1.9 collective-permute-start
  155.9 16.4 %collective-permute-done = bf16[5,4,128,128]{2,3,0,1:T(8,128)(2,1)S(1)} collective-permute-done((bf16[5,4,128,128]{2,3,0,1:T(8,128)(2,1)S(1)}, bf16[5,4,128,128]{2,3,0,1:T(8,128)(2,1)S(1)}, u32[]{:S(2)}, u32[]{:S(2)}) %collective-permute-start) | collective-permute-done | bytes 655392 | tf_op jit(solution)/shard_map/ppermute | solution.py:16
  172.2 1.1 fusion.56
  173.3 3.1 collective-permute-start.1
  176.4 16.0 %collective-permute-done.1 = bf16[5,4,128,128]{2,3,0,1:T(8,128)(2,1)S(1)} collective-permute-done((bf16[5,4,128,128]{2,3,0,1:T(8,128)(2,1)}, bf16[5,4,128,128]{2,3,0,1:T(8,128)(2,1)S(1)}, u32[]{:S(2)}, u32[]{:S(2)}) %collective-permute-start.1) | collective-permute-done | bytes 655392 | tf_op jit(solution)/shard_map/ppermute | solution.py:16
  192.4 1.1 fusion.27
  193.6 3.5 collective-permute-start.2
  197.1 101.3 %psum.7 = f32[8192]{0:T(1024)} all-reduce(f32[8192]{0:T(1024)S(1)} %get-tuple-element.6), channel_id=1, replica_groups=mesh['seq'=32,'head'=16] {'seq','head'}, use_global_device_ids=true, to_apply=%region_8.9 | all-reduce | flops 8192 | bytes 65536 | tf_op jit(solution)/shard_map/psum | solution.py:98
  298.3 2.7 multiply_reduce_fusion
  301.1 0.3 convolution_bitcast_fusion.7
  301.4 2.8 collective-permute-start.5
  304.2 2.3 fusion.26
  306.5 2.5 collective-permute-start.3
  309.0 1.2 fusion.28
  310.2 1.0 fusion.11
  311.2 3.1 collective-permute-start.6
  314.4 1.6 fusion.2
  316.0 2.0 copy.219
  318.0 5.4 %collective-permute-start.7 = (f32[64,7,4]{0,2,1:T(4,128)S(1)}, f32[64,7,4]{0,2,1:T(4,128)S(1)}, u32[]{:S(2)}, u32[]{:S(2)}) collective-permute-start(f32[64,7,4]{0,2,1:T(4,128)S(1)} %add.361), channel_id=1, source_target_pairs={{0,64},{16,80},{32,96},{48,112},{64,0},{80,16},{96,32},{112,48},{1... | collective-permute-start | bytes 21512 | tf_op jit(solution)/shard_map/ppermute | solution.py:157
  323.4 15.8 %collective-permute-done.3 = bf16[5,4,128,128]{2,3,0,1:T(8,128)(2,1)} collective-permute-done((bf16[5,4,128,128]{2,3,0,1:T(8,128)(2,1)}, bf16[5,4,128,128]{2,3,0,1:T(8,128)(2,1)}, u32[]{:S(2)}, u32[]{:S(2)}) %collective-permute-start.3) | collective-permute-done | bytes 655392 | tf_op jit(solution)/shard_map/ppermute | solution.py:16
  339.2 2.6 add_convert_fusion
  341.8 5.4 %collective-permute-start.4 = (bf16[5,4,128,128]{2,3,0,1:T(8,128)(2,1)}, bf16[5,4,128,128]{2,3,0,1:T(8,128)(2,1)}, u32[]{:S(2)}, u32[]{:S(2)}) collective-permute-start(bf16[5,4,128,128]{2,3,0,1:T(8,128)(2,1)} %add_convert_fusion), channel_id=1, source_target_pairs={{0,256},{16,272},{32,288},{48,304},{64,320},{80,336},{96,352},{112... | collective-permute-start | bytes 1966088 | tf_op jit(solution)/shard_map/ppermute | solution.py:16
  347.5 1.9 collective-permute-start.8
  349.4 1.1 slice_bitcast_fusion
  350.5 0.3 copy.226
  350.7 28.0 %collective-permute-done.8 = f32[64,7,4]{0,2,1:T(4,128)S(1)} collective-permute-done((f32[64,7,4]{0,2,1:T(4,128)S(1)}, f32[64,7,4]{0,2,1:T(4,128)S(1)}, u32[]{:S(2)}, u32[]{:S(2)}) %collective-permute-start.8) | collective-permute-done | bytes 7200 | tf_op jit(solution)/shard_map/ppermute | solution.py:157
  378.7 4.7 %collective-permute-start.9 = (f32[64,7,4]{0,2,1:T(4,128)S(1)}, f32[64,7,4]{0,2,1:T(4,128)S(1)}, u32[]{:S(2)}, u32[]{:S(2)}) collective-permute-start(f32[64,7,4]{0,2,1:T(4,128)S(1)} %add.363), channel_id=1, source_target_pairs={{0,256},{16,272},{32,288},{48,304},{64,320},{80,336},{96,352},{112... | collective-permute-start | bytes 21512 | tf_op jit(solution)/shard_map/ppermute | solution.py:157
  383.4 1.1 fusion.61
  384.8 0.7 copy.310
  385.5 1.6 collective-permute-done.9
  387.1 0.6 add.364
  388.0 1.2 convert_element_type.422
  389.2 1.2 convert_element_type.425
  390.5 1.1 fusion.31
  391.7 0.3 convolution_bitcast_fusion.2
  392.0 0.3 fusion.15
  392.3 0.3 copy-done.14
  392.6 0.3 fusion.13
  393.3 0.9 copy_bitcast_fusion
  (79 shorter events, 3.2 us)
Async XLA Ops:
  7.2 3.1 copy-start
  7.2 3.1 copy-start.20
  7.2 3.4 copy-start.18
  7.2 94.5 %all-gather.3.cloned.1.call-start = ((), (), s32[]{:S(2)}) async-start(), calls=%async_computation.2 | async-start | bytes 4325376 | tf_op jit(solution)/shard_map/all_gather | solution.py:58
  12.2 95.0 %copy-start.15 = (bf16[2,1,4,128,128]{3,4,1,2,0:T(8,128)(2,1)}, bf16[2,1,4,128,128]{3,4,1,2,0:T(8,128)(2,1)S(1)}, u32[]{:S(2)}) copy-start(bf16[2,1,4,128,128]{3,4,1,2,0:T(8,128)(2,1)S(1)} %copy.206) | copy-start | bytes 786436
  12.6 0.8 copy-start.5
  13.8 95.1 %copy-start.7 = (f32[2,128,1,4,128]{1,4,2,3,0:T(8,128)}, f32[2,128,1,4,128]{1,4,2,3,0:T(8,128)S(1)}, u32[]{:S(2)}) copy-start(f32[2,128,1,4,128]{1,4,2,3,0:T(8,128)S(1)} %convolution_bitcast_fusion.5) | copy-start | bytes 1572868
  107.2 1.1 copy-start.3
  108.9 1.7 copy-start.1
  111.3 22.5 %copy-start.17 = (bf16[16,8192]{1,0:T(8,128)(2,1)S(1)}, bf16[16,8192]{1,0:T(8,128)(2,1)}, u32[]{:S(2)}) copy-start(bf16[16,8192]{1,0:T(8,128)(2,1)} %param.13) | copy-start | bytes 786436
  111.3 22.5 %copy-start.19 = (f32[8192]{0:T(1024)S(1)}, f32[8192]{0:T(1024)}, u32[]{:S(2)}) copy-start(f32[8192]{0:T(1024)} %param.12) | copy-start | bytes 98308
  135.8 14.6 %all-to-all-start.1 = ((bf16[16,16,512]{2,0,1:T(8,128)(2,1)}), bf16[16,16,512]{2,0,1:T(8,128)(2,1)S(1)}, u32[]{:S(2)}, u32[]{:S(2)}) async-start(bf16[16,16,512]{2,0,1:T(8,128)(2,1)} %bitcast.93), calls=%async_computation.1 | async-start | bytes 524288 | tf_op jit(solution)/shard_map/all_to_all | solution.py:102
  150.4 0.7 copy-start.9
  151.4 0.8 copy-start.8
  152.2 1.6 copy-start.2
  153.9 18.3 %collective-permute-start = (bf16[5,4,128,128]{2,3,0,1:T(8,128)(2,1)S(1)}, bf16[5,4,128,128]{2,3,0,1:T(8,128)(2,1)S(1)}, u32[]{:S(2)}, u32[]{:S(2)}) collective-permute-start(bf16[5,4,128,128]{2,3,0,1:T(8,128)(2,1)S(1)} %convert_element_type.415), channel_id=1, source_target_pairs={{0,16},{16,0},{32,48},{48,32},{64,80},{80,64},{96,112},{112,96},{1... | collective-permute-start | bytes 1966088 | tf_op jit(solution)/shard_map/ppermute | solution.py:16
  173.3 19.1 %collective-permute-start.1 = (bf16[5,4,128,128]{2,3,0,1:T(8,128)(2,1)}, bf16[5,4,128,128]{2,3,0,1:T(8,128)(2,1)S(1)}, u32[]{:S(2)}, u32[]{:S(2)}) collective-permute-start(bf16[5,4,128,128]{2,3,0,1:T(8,128)(2,1)} %fusion.56), channel_id=1, source_target_pairs={{0,32},{16,48},{32,0},{48,16},{64,96},{80,112},{96,64},{112,80},{1... | collective-permute-start | bytes 1966088 | tf_op jit(solution)/shard_map/ppermute | solution.py:16
  193.6 110.6 %collective-permute-start.2 = (bf16[5,4,128,128]{2,3,0,1:T(8,128)(2,1)}, bf16[5,4,128,128]{2,3,0,1:T(8,128)(2,1)}, u32[]{:S(2)}, u32[]{:S(2)}) collective-permute-start(bf16[5,4,128,128]{2,3,0,1:T(8,128)(2,1)} %fusion.27), channel_id=1, source_target_pairs={{0,64},{16,80},{32,96},{48,112},{64,0},{80,16},{96,32},{112,48},{1... | collective-permute-start | bytes 1966088 | tf_op jit(solution)/shard_map/ppermute | solution.py:16
  301.4 7.6 %copy-start.6 = (f32[2,4,128,128]{3,2,1,0:T(8,128)S(1)}, f32[2,4,128,128]{3,2,1,0:T(8,128)}, u32[]{:S(2)}) copy-start(f32[2,4,128,128]{3,2,1,0:T(8,128)} %copy-done.5) | copy-start | bytes 1572868
  301.4 7.6 %copy-start.10 = (bf16[2,128,4,128]{3,2,1,0:T(4,128)(2,1)S(1)}, bf16[2,128,4,128]{3,2,1,0:T(4,128)(2,1)}, u32[]{:S(2)}) copy-start(bf16[2,128,4,128]{3,2,1,0:T(4,128)(2,1)} %copy-done.9) | copy-start | bytes 786436
  301.4 9.8 %collective-permute-start.5 = (f32[64,7,4]{0,2,1:T(4,128)S(1)}, f32[64,7,4]{0,2,1:T(4,128)S(1)}, u32[]{:S(2)}, u32[]{:S(2)}) collective-permute-start(f32[64,7,4]{0,2,1:T(4,128)S(1)} %convolution_bitcast_fusion.7), channel_id=1, source_target_pairs={{0,16},{16,0},{32,48},{48,32},{64,80},{80,64},{96,112},{112,96},{1... | collective-permute-start | bytes 21512 | tf_op jit(solution)/shard_map/ppermute | solution.py:157
  306.5 7.8 %copy-start.4 = (bf16[2,5,4,128,128]{3,4,1,2,0:T(8,128)(2,1)S(1)}, bf16[2,5,4,128,128]{3,4,1,2,0:T(8,128)(2,1)}, u32[]{:S(2)}) copy-start(bf16[2,5,4,128,128]{3,4,1,2,0:T(8,128)(2,1)} %copy-done.3) | copy-start | bytes 3932164
  306.5 7.8 %copy-start.16 = (bf16[2,1,4,128,128]{3,4,1,2,0:T(8,128)(2,1)S(1)}, bf16[2,1,4,128,128]{3,4,1,2,0:T(8,128)(2,1)}, u32[]{:S(2)}) copy-start(bf16[2,1,4,128,128]{3,4,1,2,0:T(8,128)(2,1)} %copy-done.15) | copy-start | bytes 786436
  306.5 32.7 %collective-permute-start.3 = (bf16[5,4,128,128]{2,3,0,1:T(8,128)(2,1)}, bf16[5,4,128,128]{2,3,0,1:T(8,128)(2,1)}, u32[]{:S(2)}, u32[]{:S(2)}) collective-permute-start(bf16[5,4,128,128]{2,3,0,1:T(8,128)(2,1)} %fusion.26), channel_id=1, source_target_pairs={{0,128},{16,144},{32,160},{48,176},{64,192},{80,208},{96,224},{112... | collective-permute-start | bytes 1966088 | tf_op jit(solution)/shard_map/ppermute | solution.py:16
  311.2 6.7 %collective-permute-start.6 = (f32[64,7,4]{0,2,1:T(4,128)S(1)}, f32[64,7,4]{0,2,1:T(4,128)S(1)}, u32[]{:S(2)}, u32[]{:S(2)}) collective-permute-start(f32[64,7,4]{0,2,1:T(4,128)S(1)} %add.360), channel_id=1, source_target_pairs={{0,32},{16,48},{32,0},{48,16},{64,96},{80,112},{96,64},{112,80},{1... | collective-permute-start | bytes 21512 | tf_op jit(solution)/shard_map/ppermute | solution.py:157
  318.0 29.2 %copy-start.12 = (f32[2,128,4,128]{3,1,2,0:T(8,128)S(1)}, f32[2,128,4,128]{3,1,2,0:T(8,128)}, u32[]{:S(2)}) copy-start(f32[2,128,4,128]{3,1,2,0:T(8,128)} %copy.219) | copy-start | bytes 1572868
  318.0 29.2 %copy-start.13 = (bf16[2,4,128,128]{3,2,1,0:T(8,128)(2,1)S(1)}, bf16[2,4,128,128]{3,2,1,0:T(8,128)(2,1)}, u32[]{:S(2)}) copy-start(bf16[2,4,128,128]{3,2,1,0:T(8,128)(2,1)} %fusion.11) | copy-start | bytes 786436
  318.0 29.4 %collective-permute-start.7 = (f32[64,7,4]{0,2,1:T(4,128)S(1)}, f32[64,7,4]{0,2,1:T(4,128)S(1)}, u32[]{:S(2)}, u32[]{:S(2)}) collective-permute-start(f32[64,7,4]{0,2,1:T(4,128)S(1)} %add.361), channel_id=1, source_target_pairs={{0,64},{16,80},{32,96},{48,112},{64,0},{80,16},{96,32},{112,48},{1... | collective-permute-start | bytes 21512 | tf_op jit(solution)/shard_map/ppermute | solution.py:157
  341.8 48.6 %collective-permute-start.4 = (bf16[5,4,128,128]{2,3,0,1:T(8,128)(2,1)}, bf16[5,4,128,128]{2,3,0,1:T(8,128)(2,1)}, u32[]{:S(2)}, u32[]{:S(2)}) collective-permute-start(bf16[5,4,128,128]{2,3,0,1:T(8,128)(2,1)} %add_convert_fusion), channel_id=1, source_target_pairs={{0,256},{16,272},{32,288},{48,304},{64,320},{80,336},{96,352},{112... | collective-permute-start | bytes 1966088 | tf_op jit(solution)/shard_map/ppermute | solution.py:16
  347.5 31.3 %collective-permute-start.8 = (f32[64,7,4]{0,2,1:T(4,128)S(1)}, f32[64,7,4]{0,2,1:T(4,128)S(1)}, u32[]{:S(2)}, u32[]{:S(2)}) collective-permute-start(f32[64,7,4]{0,2,1:T(4,128)S(1)} %add.362), channel_id=1, source_target_pairs={{0,128},{16,144},{32,160},{48,176},{64,192},{80,208},{96,224},{112... | collective-permute-start | bytes 21512 | tf_op jit(solution)/shard_map/ppermute | solution.py:157
  378.7 8.4 %collective-permute-start.9 = (f32[64,7,4]{0,2,1:T(4,128)S(1)}, f32[64,7,4]{0,2,1:T(4,128)S(1)}, u32[]{:S(2)}, u32[]{:S(2)}) collective-permute-start(f32[64,7,4]{0,2,1:T(4,128)S(1)} %add.363), channel_id=1, source_target_pairs={{0,256},{16,272},{32,288},{48,304},{64,320},{80,336},{96,352},{112... | collective-permute-start | bytes 21512 | tf_op jit(solution)/shard_map/ppermute | solution.py:157
  390.4 1.5 copy-start.11
  391.7 1.0 copy-start.14
Sparse Core Ops, SparseCore 0:
  11.8 89.9 all-gather.2
